TPU v7x, 32 devices: a whole 2x2x4 slice. The times are simulated.
32 devices in a mesh: grp: 2 (over y), dec: 4 (over z), stg: 2 (over x), tp: 2 (over core).
Axes of the slice: x: 2, y: 2, z: 4, core: 2. Of those that a mesh axis runs over, the one named last changes fastest.
Arguments:
- hidden_x: bfloat16 [3072, 7168], P(('grp', 'dec'), ('stg', 'tp')), parts along dimension 0, may hold values from -8 to 8
- proj_weight: bfloat16 [7168, 2112], P(('stg', 'tp'), 'dec'), may hold values from -0.0625 to 0.0625
- q_gain: float32 [1536], replicated, may hold values from 0.25 to 1.75
- kv_gain: float32 [512], replicated, may hold values from 0.25 to 1.75
- old_cache: bfloat16 [256, 32, 576], P(('grp', 'dec')), parts along dimension 0, may hold values from -6 to 6
- page_plan: int32 [96, 2], P(('grp', 'dec')), parts along dimension 0, may hold values from 0 to 31, as said below
- block_table: int32 [8, 4, 8], P(('grp', 'dec')), parts along dimension 0, may hold values from 0 to 31, as said below
- split_lens: int32 [8, 4], P('grp', 'dec'), parts along dimension 0, may hold values from 2 to 256, as said below
- dec_query: bfloat16 [8, 128, 576], P('grp', ('stg', 'tp')), parts along dimension 0, may hold values from -66 to 66
- new_key: bfloat16 [8, 576], P('grp'), parts along dimension 0, may hold values from -12 to 12
Outputs:
- q_latent: bfloat16 [3072, 1536], P(('grp', 'dec'), ('stg', 'tp')), parts along dimension 0
- attn_latent: bfloat16 [8, 128, 512], P('grp', ('stg', 'tp')), parts along dimension 0
There are 2 independent parts, one for each index of `grp`. A program takes and returns all parts, laid end to end along the dimension named above; an argument that names none is the same for every part. Nothing has to cross between parts.
Inputs may be any that keep to these rules, and one draw needn't show every extreme that they name: `page_plan`: column 0 is the owner of prefill page g, column 1 its slot among the owner's 32; no two pages share owner and slot; in each aligned block of 12 rows (one index of dec) no owner appears more than 3 times and some owner exactly 3 times; no page goes to a slot block_table[o, r, 0]. `block_table`: for each owner the 4 x 8 entries are its 32 slots, each once. `split_lens`: each request has exactly 256 tokens on at least one owner.
All inputs are finite; a program needn't handle non-finite values.
Results may differ from a plain program's by a relative error of at most 0.0054.
Values may be sent and summed in bfloat16 or wider, within the bound.
A program may use at most 64 MiB of HBM per device.

v0:
```python
import jax
import jax.numpy as jnp
from jax import lax
from jax.sharding import PartitionSpec as P

QL = 1536
KVL = 512
ROPE = 64
PAGE = 32


softmax_scale = 192.0 ** (-0.5)
norm_eps = 1e-06


def combined_all(part, axis, combine):
    gathered = jax.tree.map(lambda a: lax.all_gather(a, axis), part)

    def take(source):
        return jax.tree.map(lambda a: lax.dynamic_index_in_dim(a, source, 0, False), gathered)

    return lax.fori_loop(
        1, lax.axis_size(axis), lambda source, state: combine(state, take(source)), take(0)
    )


def rope_rotate(matrix, col_start, positions):
    col_count = matrix.shape[1]
    columns = col_start + jnp.arange(col_count, dtype=jnp.int32)
    is_rope = columns >= KVL
    pair_index = jnp.maximum(columns - KVL, 0) // 2
    frequency = jnp.power(jnp.float32(10000.0), -(2 * pair_index).astype(jnp.float32) / ROPE)
    angles = positions[:, None] * frequency[None, :]
    cosine = jnp.where(is_rope[None, :], jnp.cos(angles), 1.0)
    sine_part = jnp.where(is_rope[None, :], jnp.sin(angles), 0.0)
    paired = matrix.reshape(matrix.shape[0], col_count // 2, 2)
    partner = jnp.stack([-paired[:, :, 1], paired[:, :, 0]], axis=2).reshape(matrix.shape)
    return matrix * cosine + partner * sine_part


def kv_finish(matrix, col_start, latent_sq, kv_gain, positions):
    col_count = matrix.shape[1]
    columns = col_start + jnp.arange(col_count, dtype=jnp.int32)
    gain_full = jnp.concatenate([kv_gain, jnp.ones((ROPE,), jnp.float32)])
    gain_cols = lax.dynamic_slice_in_dim(gain_full, col_start, col_count)
    inverse = lax.rsqrt(latent_sq / KVL + norm_eps)
    row_scale = jnp.where(columns[None, :] < KVL, inverse[:, None] * gain_cols[None, :], 1.0)
    return rope_rotate(matrix * row_scale, col_start, positions).astype(jnp.bfloat16)


def pack_pages(kv_pages, page_table, owner_count, capacity):
    owners = page_table[:, 0]
    slot_ids = page_table[:, 1]
    page_ids = jnp.arange(kv_pages.shape[0], dtype=jnp.int32)
    earlier = (owners[:, None] == owners[None, :]) & (page_ids[None, :] < page_ids[:, None])
    ranking = jnp.sum(earlier.astype(jnp.int32), axis=1)
    targets = owners * capacity + ranking
    places = jnp.arange(owner_count * capacity, dtype=jnp.int32)
    matches = targets[None, :] == places[:, None]
    source_ids = jnp.sum(jnp.where(matches, page_ids[None, :], 0), axis=1)
    filled = jnp.any(matches, axis=1)
    chosen = jnp.where(
        filled[:, None, None], jnp.take(kv_pages, source_ids, axis=0), jnp.zeros((), kv_pages.dtype)
    )
    labels = jnp.where(filled, jnp.take(slot_ids, source_ids), -1).astype(jnp.bfloat16)
    return (
        chosen.reshape(owner_count, capacity, kv_pages.shape[1], kv_pages.shape[2]),
        labels.reshape(owner_count, capacity),
    )


def place_pages(old_cache, got_pages, got_labels):
    flat_pages = got_pages.reshape(-1, old_cache.shape[1], old_cache.shape[2])
    label_ids = got_labels.reshape(-1).astype(jnp.int32)
    slot_ids = jnp.arange(old_cache.shape[0], dtype=jnp.int32)
    arrival_ids = jnp.arange(label_ids.shape[0], dtype=jnp.int32)
    matches = label_ids[None, :] == slot_ids[:, None]
    source_ids = jnp.sum(jnp.where(matches, arrival_ids[None, :], 0), axis=1)
    arrived = jnp.any(matches, axis=1)
    return jnp.where(arrived[:, None, None], jnp.take(flat_pages, source_ids, axis=0), old_cache)


def combine_parts(former, latter):
    overall = jnp.maximum(former[0], latter[0])
    front_scale = jnp.exp(former[0] - overall)
    back_scale = jnp.exp(latter[0] - overall)
    return (
        overall,
        former[1] * front_scale + latter[1] * back_scale,
        former[2] * front_scale[:, :, None] + latter[2] * back_scale[:, :, None],
    )


def body(
    hidden_x,
    proj_weight,
    q_gain,
    kv_gain,
    old_cache,
    page_plan,
    block_table,
    split_lens,
    dec_query,
    new_key,
):
    projected = jnp.dot(
        hidden_x,
        lax.all_gather(proj_weight, "dec", axis=1, tiled=True),
        preferred_element_type=jnp.float32,
    )
    query_part = projected[:, :QL]
    kv_part = projected[:, QL:]
    tokens_here = hidden_x.shape[0]
    positions = (
        lax.axis_index("dec") * tokens_here + jnp.arange(tokens_here, dtype=jnp.int32)
    ).astype(jnp.float32)
    lane_count = lax.axis_size(("stg", "tp"))
    lane_index = lax.axis_index(("stg", "tp"))
    owner_count = lax.axis_size("dec")
    page_count = page_plan.shape[0]
    capacity = max(2, -(-page_count // owner_count))
    query_width = QL // lane_count
    query_cols, kv_cols = (
        lax.psum_scatter(query_part, ("stg", "tp"), scatter_dimension=1, tiled=True),
        lax.psum_scatter(kv_part, ("stg", "tp"), scatter_dimension=1, tiled=True),
    )
    kv_width = kv_cols.shape[1]
    col_start = lane_index * kv_width
    columns = col_start + jnp.arange(kv_width, dtype=jnp.int32)
    latent_part_sq = jnp.sum(jnp.where(columns[None, :] < KVL, kv_cols * kv_cols, 0.0), axis=1)
    query_sq, latent_sq = lax.psum(
        (jnp.sum(query_cols * query_cols, axis=1), latent_part_sq), ("stg", "tp")
    )
    kv_rows = kv_finish(kv_cols, col_start, latent_sq, kv_gain, positions)
    kv_pages = kv_rows.reshape(page_count, PAGE, kv_width)
    send_pages, send_labels = pack_pages(kv_pages, page_plan, owner_count, capacity)
    got_slices, got_labels = (
        lax.all_to_all(send_pages, "dec", split_axis=0, concat_axis=0, tiled=True),
        lax.all_to_all(send_labels, "dec", split_axis=0, concat_axis=0, tiled=True),
    )
    got_pages = lax.all_gather(got_slices, ("stg", "tp"), axis=3, tiled=True)
    query_gain = lax.dynamic_slice_in_dim(q_gain, lane_index * query_width, query_width)
    q_latent = (
        query_cols * lax.rsqrt(query_sq / QL + norm_eps)[:, None] * query_gain[None, :]
    ).astype(jnp.bfloat16)
    cache = place_pages(old_cache, got_pages, got_labels)
    slot_table = block_table[0]
    request_count = slot_table.shape[0]
    key_rows = jnp.take(cache, slot_table.reshape(-1), axis=0).reshape(
        request_count, -1, cache.shape[2]
    )
    scores = (
        jnp.einsum("rhc,rlc->rhl", dec_query, key_rows, preferred_element_type=jnp.float32)
        * softmax_scale
    )
    live_mask = jnp.arange(key_rows.shape[1], dtype=jnp.int32)[None, :] < split_lens[:, 0][:, None]
    scores = jnp.where(live_mask[:, None, :], scores, -1e30)
    row_peak = jnp.max(scores, axis=2)
    weights = jnp.where(live_mask[:, None, :], jnp.exp(scores - row_peak[:, :, None]), 0.0)
    row_total = jnp.sum(weights, axis=2)
    rounded = weights.astype(jnp.bfloat16)
    partial_out = jnp.einsum(
        "rhl,rlc->rhc", rounded, key_rows[:, :, :KVL], preferred_element_type=jnp.float32
    )
    peak_all, total_all, output_all = combined_all(
        (row_peak, row_total, partial_out), "dec", combine_parts
    )
    self_score = (
        jnp.einsum("rhc,rc->rh", dec_query, new_key, preferred_element_type=jnp.float32)
        * softmax_scale
    )
    overall = jnp.maximum(peak_all, self_score)
    carried = jnp.exp(peak_all - overall)
    self_weight = jnp.exp(self_score - overall)
    denom = total_all * carried + self_weight
    numer = output_all * carried[:, :, None] + self_weight[:, :, None] * new_key[
        :, None, :KVL
    ].astype(jnp.float32)
    attn_latent = (numer / denom[:, :, None]).astype(jnp.bfloat16)
    return (q_latent, attn_latent)


def solution(mesh):
    return jax.shard_map(
        body,
        mesh=mesh,
        in_specs=(
            P(("grp", "dec"), ("stg", "tp")),
            P(("stg", "tp"), "dec"),
            P(),
            P(),
            P(("grp", "dec"), None, None),
            P(("grp", "dec"), None),
            P(("grp", "dec"), None, None),
            P("grp", "dec"),
            P("grp", ("stg", "tp"), None),
            P("grp", None),
        ),
        out_specs=(P(("grp", "dec"), ("stg", "tp")), P("grp", ("stg", "tp"), None)),
        check_vma=False,
    )
```

profile of v0, /device:TPU:0, one launch (start us, length us, event | category | flops | bytes accessed | tf_op | source)
XLA Modules:
  0.0 303.2 jit_solution(6917555264562999313)
XLA Ops:
  8.0 140.6 %all-gather.8.cloned.1.call-done = bf16[1792,2112]{0,1:T(8,128)(2,1)} async-done(((bf16[1792,528]{0,1:T(8,128)(2,1)}), bf16[1792,2112]{0,1:T(8,128)(2,1)}) %all-gather.8.cloned.1.call-update) | async-done | bytes 7569424 | tf_op jit(solution)/shard_map/all_gather | solution.py:108
  148.5 6.4 %fusion.36 = f32[384,2112]{0,1:T(8,128)S(1)} fusion(bf16[384,1792]{1,0:T(8,128)(2,1)S(1)} %copy-done, bf16[1792,2112]{0,1:T(8,128)(2,1)} %all-gather.8.cloned.1.call-done), kind=kOutput, calls=%fused_computation.93 | convolution fusion | flops 2906652672 | bytes 12189696 | tf_op jit(solution)/shard_map/dot_general | solution.py:106
  155.0 1.7 copy-done.1
  157.7 3.3 %slice.48 = f32[384,1536]{0,1:T(8,128)} slice(f32[384,2112]{0,1:T(8,128)} %copy-done.1), slice={[0:384], [0:1536]} | slice | bytes 4718592 | tf_op jit(solution)/shard_map/slice | solution.py:111
  163.6 3.2 %all-to-all-start = ((bf16[4,1,3]{2,1,0:T(2,128)(2,1)}), bf16[4,1,3]{2,1,0:T(2,128)(2,1)S(1)}, u32[]{:S(2)}, u32[]{:S(2)}) async-start(bf16[4,1,3]{2,1,0:T(2,128)(2,1)} %copy.23), calls=%async_computation.1 | async-start | bytes 4096 | tf_op jit(solution)/shard_map/all_to_all | solution.py:139
  167.5 4.8 %all-to-all-done = bf16[4,1,3]{2,1,0:T(2,128)(2,1)S(1)} async-done(((bf16[4,1,3]{2,1,0:T(2,128)(2,1)}), bf16[4,1,3]{2,1,0:T(2,128)(2,1)S(1)}, u32[]{:S(2)}, u32[]{:S(2)}) %all-to-all-start) | async-done | bytes 56 | tf_op jit(solution)/shard_map/all_to_all | solution.py:139
  172.5 7.3 %reduce-scatter.5.cloned.1.call-done = f32[384,144]{0,1:T(8,128)} async-done(((f32[384,576]{0,1:T(8,128)}), f32[384,144]{0,1:T(8,128)}) %reduce-scatter.5.cloned.1.call-update) | async-done | bytes 221200 | tf_op jit(solution)/shard_map/reduce_scatter | solution.py:125
  180.8 34.3 %reduce-scatter.3.cloned.1.call-done = f32[384,384]{0,1:T(8,128)} async-done(((f32[384,1536]{0,1:T(8,128)}), f32[384,384]{0,1:T(8,128)}) %reduce-scatter.3.cloned.1.call-update) | async-done | bytes 589840 | tf_op jit(solution)/shard_map/reduce_scatter | solution.py:124
  215.2 1.1 multiply_reduce_fusion
  216.3 5.8 %all-reduce.1 = (f32[384]{0:T(512)S(1)}, f32[384]{0:T(512)S(1)}) all-reduce(f32[384]{0:T(512)S(1)} %multiply_reduce_fusion, f32[384]{0:T(512)S(1)} %select_reduce_fusion), channel_id=1, replica_groups=mesh['grp'=2,'dec'=4,'stg'=2,'tp'=2] {'stg','tp'}, use_global_device_ids=true, to_apply=%region_2.3 | all-reduce | flops 768 | bytes 6144 | tf_op jit(solution)/shard_map/psum | solution.py:131
  223.8 1.1 fusion.10
  226.4 4.8 %all-to-all-start.1 = ((bf16[4,3,32,144]{3,2,1,0:T(8,128)(2,1)}), bf16[4,3,32,144]{3,2,1,0:T(8,128)(2,1)S(1)}, u32[]{:S(2)}, u32[]{:S(2)}) async-start(bf16[4,3,32,144]{3,2,1,0:T(8,128)(2,1)} %select_select_fusion.1), calls=%async_computation.3 | async-start | bytes 393216 | tf_op jit(solution)/shard_map/all_to_all | solution.py:138
  231.3 7.2 %all-to-all-done.1 = bf16[4,3,32,144]{3,2,1,0:T(8,128)(2,1)S(1)} async-done(((bf16[4,3,32,144]{3,2,1,0:T(8,128)(2,1)}), bf16[4,3,32,144]{3,2,1,0:T(8,128)(2,1)S(1)}, u32[]{:S(2)}, u32[]{:S(2)}) %all-to-all-start.1) | async-done | bytes 110624 | tf_op jit(solution)/shard_map/all_to_all | solution.py:138
  239.5 13.5 %all_gather.25 = bf16[4,3,32,576]{2,0,1,3:T(4,128)(2,1)S(1)} all-gather(bf16[4,3,32,144]{2,0,1,3:T(4,128)(2,1)} %copy.25), channel_id=1, replica_groups=mesh['grp'=2,'dec'=4,'stg'=2,'tp'=2] {'stg','tp'}, dimensions={3}, use_global_device_ids=true | all-gather | bytes 552960 | tf_op jit(solution)/shard_map/all_gather | solution.py:141
  253.0 2.4 copy.26
  255.4 1.8 gather_fusion.2
  257.2 2.7 select_select_fusion
  259.9 2.1 gather_fusion.3
  266.6 12.2 %all-gather.3 = f32[4,4,32]{2,1,0:T(4,128)S(1)} all-gather(f32[1,4,32]{2,1,0:T(4,128)S(1)} %bitcast.72), channel_id=2, replica_groups=mesh['grp'=2,'dec'=4,'stg'=2,'tp'=2] {'dec'}, dimensions={0}, use_global_device_ids=true | all-gather | bytes 2560 | tf_op jit(solution)/shard_map/all_gather | solution.py:17
  278.9 12.3 %all-gather.4 = f32[4,4,32]{2,1,0:T(4,128)S(1)} all-gather(f32[1,4,32]{2,1,0:T(4,128)S(1)} %bitcast.73), channel_id=3, replica_groups=mesh['grp'=2,'dec'=4,'stg'=2,'tp'=2] {'dec'}, dimensions={0}, use_global_device_ids=true | all-gather | bytes 2560 | tf_op jit(solution)/shard_map/all_gather | solution.py:17
  292.5 3.4 %while.19 = (s32[]{:T(128)}, f32[4,32]{1,0:T(4,128)S(1)}, f32[4,32]{1,0:T(4,128)S(1)}, f32[4,32,512]{2,1,0:T(8,128)S(1)}, f32[4,4,32]{2,1,0:T(4,128)S(1)}, /*ind...) while((s32[]{:T(128)}, f32[4,32]{1,0:T(4,128)S(1)}, ...), condition=%wide.region_14.15_spmd, body=%wide.region_13.14_spmd.sunk | while | flops 197381 | bytes 791703 | solution.py:22
  292.6 1.1 fusion.45
  293.7 1.1 fusion.45
  294.8 1.1 fusion.45
  (92 shorter events, 17.5 us)
Async XLA Ops:
  7.2 141.4 %copy-start = (bf16[384,1792]{1,0:T(8,128)(2,1)S(1)}, bf16[384,1792]{1,0:T(8,128)(2,1)}, u32[]{:S(2)}) copy-start(bf16[384,1792]{1,0:T(8,128)(2,1)} %param.12) | copy-start | bytes 4128772
  7.2 141.4 %all-gather.8.cloned.1.call-start = ((), (), s32[]{:S(2)}) async-start(), calls=%async_computation.4 | async-start | bytes 9461760 | tf_op jit(solution)/shard_map/all_gather | solution.py:108
  7.9 171.9 %reduce-scatter.5.cloned.1.call-start = ((), (), s32[]{:S(2)}) async-start(), calls=%async_computation.6 | async-start | bytes 1105920 | tf_op jit(solution)/shard_map/reduce_scatter | solution.py:125
  154.9 1.7 copy-start.1
  157.6 57.5 %reduce-scatter.3.cloned.1.call-start = ((), (), s32[]{:S(2)}) async-start(), calls=%async_computation.5 | async-start | bytes 2949120 | tf_op jit(solution)/shard_map/reduce_scatter | solution.py:124
  160.9 0.7 copy-start.8
  161.0 6.1 %copy-start.5 = (s32[1,4,8]{2,1,0:T(4,128)S(1)}, s32[1,4,8]{2,1,0:T(4,128)}, u32[]{:S(2)}) copy-start(s32[1,4,8]{2,1,0:T(4,128)} %param.18) | copy-start | bytes 388
  161.0 6.4 %copy-start.7 = (f32[512]{0:T(512)S(1)}, f32[512]{0:T(512)}, u32[]{:S(2)}) copy-start(f32[512]{0:T(512)} %param.15) | copy-start | bytes 6148
  161.0 6.5 %copy-start.9 = (s32[4,1]{0,1:T(1,128)S(1)}, s32[4,1]{0,1:T(1,128)}, u32[]{:S(2)}) copy-start(s32[4,1]{0,1:T(1,128)} %param.19) | copy-start | bytes 52
  163.6 8.7 %all-to-all-start = ((bf16[4,1,3]{2,1,0:T(2,128)(2,1)}), bf16[4,1,3]{2,1,0:T(2,128)(2,1)S(1)}, u32[]{:S(2)}, u32[]{:S(2)}) async-start(bf16[4,1,3]{2,1,0:T(2,128)(2,1)} %copy.23), calls=%async_computation.1 | async-start | bytes 4096 | tf_op jit(solution)/shard_map/all_to_all | solution.py:139
  180.8 43.0 %copy-start.3 = (f32[384,144]{0,1:T(8,128)S(1)}, f32[384,144]{0,1:T(8,128)}, u32[]{:S(2)}) copy-start(f32[384,144]{0,1:T(8,128)} %reduce-scatter.5.cloned.1.call-done) | copy-start | bytes 663556
  226.4 12.1 %all-to-all-start.1 = ((bf16[4,3,32,144]{3,2,1,0:T(8,128)(2,1)}), bf16[4,3,32,144]{3,2,1,0:T(8,128)(2,1)S(1)}, u32[]{:S(2)}, u32[]{:S(2)}) async-start(bf16[4,3,32,144]{3,2,1,0:T(8,128)(2,1)} %select_select_fusion.1), calls=%async_computation.3 | async-start | bytes 393216 | tf_op jit(solution)/shard_map/all_to_all | solution.py:138
  231.2 60.3 %all-gather.10.cloned.1.call-start = ((), (), s32[]{:S(2)}) async-start(), calls=%async_computation.7 | async-start | bytes 1310720 | tf_op jit(solution)/shard_map/all_gather | solution.py:17
  262.0 0.9 copy-start.4
  262.9 2.5 copy-start.6
  263.5 2.0 copy-start.2
Sparse Core Ops, SparseCore 0:
  9.6 138.9 all-gather.7
  157.8 21.9 reduce-scatter.4
  182.3 32.7 reduce-scatter.2
  264.7 26.8 all-gather.9
where the time goes:
time: 304 us; the launch traced here: 303 us
  waiting for transfers between devices  195 us (64%)
  blocking collectives  43.7 us (14%)
  local copies, waits for them, and re-layouts  20.2 us (7%)
  between operations  14 us (5%)
  other arithmetic  13.6 us (4%)
  matrix products  8.18 us (3%)
  starting transfers between devices  8.14 us (3%)
    all_gather x1, waiting for transfers between devices, body(): lax.all_gather(proj_weight, 'dec', axis=1, tiled=True)  141 us
    reduce_scatter x1, waiting for transfers between devices, body(): lax.psum_scatter(query_part, ('stg', 'tp'), scatter_dimension=1, tiled=True)  34.3 us
    all_gather x2, blocking collectives, combined_all(): gathered = jax.tree.map(lambda a: lax.all_gather(a, axis), part)  24.5 us
    all_gather x1, blocking collectives, body(): got_pages = lax.all_gather(got_slices, ('stg', 'tp'), axis=3, tiled=True)  13.5 us
    reduce_scatter x1, waiting for transfers between devices, body(): lax.psum_scatter(kv_part, ('stg', 'tp'), scatter_dimension=1, tiled=True)  7.27 us
    all_to_all x1, waiting for transfers between devices, body(): lax.all_to_all(send_pages, 'dec', split_axis=0, concat_axis=0, tiled=True)  7.2 us
    dot_general x1, matrix products, body(): jnp.dot(hidden_x, lax.all_gather(proj_weight, 'dec', axis=1, tiled=True),...  6.4 us
  transfers between devices with their start and end apart: 6, of which 6 were waited for; matrix products, arithmetic and copies ran while one was open for 3% of the time, Pallas kernels for 0%

commit v1 on v0

--- a/solution.py
+++ b/solution.py
@@ -1,6 +1,10 @@
+import functools
+
 import jax
 import jax.numpy as jnp
 from jax import lax
+from jax.experimental import pallas as pl
+from jax.experimental.pallas import tpu as pltpu
 from jax.sharding import PartitionSpec as P
 
 QL = 1536
@@ -91,6 +95,286 @@
     )
 
 
+MESH = pl.DeviceIdType.MESH
+
+
+def proj_kernel(
+    dims, w_ref, x_ref, qg_ref, kg_ref, cos_ref, sin_ref, q_out, k_out,
+    wbuf, pt, aq, bq, bk, cq, ck, eq, ek, ss, ssin,
+    zsem, zrecv, ysem, yrecv, t_send, t_recv, s_send, s_recv, v_send, v_recv,
+):
+    D, G, S, T, K = dims
+    C, fg = w_ref.shape[1], w_ref.shape[2]
+    qw, kw = qg_ref.shape[0], kg_ref.shape[0]
+    ck_rows = C // K
+    me, g = lax.axis_index("dec"), lax.axis_index("grp")
+    st, tp = lax.axis_index("stg"), lax.axis_index("tp")
+
+    barrier = pltpu.get_barrier_semaphore()
+
+    def greet(target):
+        pl.semaphore_signal(barrier, inc=1, device_id=target, device_id_type=MESH)
+
+    @pl.when(me > 0)
+    def _():
+        greet({"dec": me - 1})
+
+    @pl.when(me < D - 1)
+    def _():
+        greet({"dec": me + 1})
+
+    for d in range(1, G):
+        greet({"grp": lax.rem(g + d, G)})
+    lane_steps = [(a, b) for a in range(S) for b in range(T) if a or b]
+
+    def lane_at(a, b):
+        return {"stg": lax.rem(st + a, S), "tp": lax.rem(tp + b, T)}
+
+    for a, b in lane_steps:
+        greet(lane_at(a, b))
+    ends = (me > 0).astype(jnp.int32) + (me < D - 1).astype(jnp.int32)
+    pl.semaphore_wait(barrier, ends + (G - 1) + len(lane_steps))
+
+    def chunk(ref, j, part, c):
+        return ref.at[j, part, pl.ds(c * ck_rows, ck_rows)]
+
+    def z_copy(j, c, way, own):
+        src = w_ref.at[g, pl.ds(c * ck_rows, ck_rows)] if own else chunk(wbuf, j, g, c)
+        to = me + 1 if way == 0 else me - 1
+        return pltpu.make_async_remote_copy(
+            src_ref=src, dst_ref=chunk(wbuf, j, g, c),
+            send_sem=zsem.at[way, j, c], recv_sem=zrecv.at[j, c],
+            device_id={"dec": to}, device_id_type=MESH,
+        )
+
+    def y_copy(j, c, d):
+        return pltpu.make_async_remote_copy(
+            src_ref=chunk(wbuf, j, g, c), dst_ref=chunk(wbuf, j, g, c),
+            send_sem=ysem.at[d - 1, j, c], recv_sem=yrecv.at[d - 1, j, c],
+            device_id={"grp": lax.rem(g + d, G)}, device_id_type=MESH,
+        )
+
+    def y_arrive(j, c, d):
+        part = lax.rem(g + G - d, G)
+        return pltpu.make_async_remote_copy(
+            src_ref=chunk(wbuf, j, part, c), dst_ref=chunk(wbuf, j, part, c),
+            send_sem=ysem.at[d - 1, j, c], recv_sem=yrecv.at[d - 1, j, c],
+            device_id={"grp": part}, device_id_type=MESH,
+        )
+
+    def can_send(way):
+        return me < D - 1 if way == 0 else me > 0
+
+    def sides(s):
+        left, right = me - s, me + s
+        return ((0, left, left >= 0), (1, right, right <= D - 1))
+
+    for c in range(K):
+        for way in (0, 1):
+            @pl.when(can_send(way))
+            def _():
+                z_copy(me, c, way, True).start()
+
+    def project(weights, j):
+        total = None
+        for part in range(G):
+            term = lax.dot_general(
+                weights(part), x_ref[:, part * fg : (part + 1) * fg],
+                (((1,), (1,)), ((), ())), preferred_element_type=jnp.float32,
+            )
+            total = term if total is None else total + term
+        pt[pl.ds(pl.multiple_of(j * C, 16), C), :] = total
+
+    project(lambda part: w_ref[part], me)
+
+    def finish_round(s):
+        for way, j, there in sides(s):
+            @pl.when(there)
+            def _():
+                for c in range(K):
+                    for d in range(1, G):
+                        y_arrive(j, c, d).wait_recv()
+                project(lambda part: wbuf[j, part], j)
+
+    for s in range(1, D):
+        for c in range(K):
+            for way, j, there in sides(s):
+                @pl.when(there)
+                def _():
+                    z_copy(j, c, way, False).wait_recv()
+                    for d in range(1, G):
+                        y_copy(j, c, d).start()
+
+                @pl.when(there & can_send(way))
+                def _():
+                    z_copy(j, c, way, False).start()
+        if s > 1:
+            finish_round(s - 1)
+    finish_round(D - 1)
+
+    def q_rows(lane):
+        return pt[pl.ds(pl.multiple_of(lane * qw, 16), qw), :]
+
+    def k_view(lane):
+        return pt.at[pl.ds(pl.multiple_of(QL + lane * kw, 16), kw)]
+
+    copies = []
+    for d in range(1, T):
+        t2 = lax.rem(tp + d, T)
+        for a in range(S):
+            kcopy = pltpu.make_async_remote_copy(
+                src_ref=k_view(a * T + t2), dst_ref=bk.at[d - 1, a],
+                send_sem=t_send.at[0, d - 1, a], recv_sem=t_recv.at[0, d - 1, a],
+                device_id={"tp": t2}, device_id_type=MESH,
+            )
+            kcopy.start()
+            aq[d - 1, a] = q_rows(a * T + t2).astype(jnp.bfloat16)
+            qcopy = pltpu.make_async_remote_copy(
+                src_ref=aq.at[d - 1, a], dst_ref=bq.at[d - 1, a],
+                send_sem=t_send.at[1, d - 1, a], recv_sem=t_recv.at[1, d - 1, a],
+                device_id={"tp": t2}, device_id_type=MESH,
+            )
+            qcopy.start()
+            copies += [kcopy, qcopy]
+    for copy in copies:
+        copy.wait_recv()
+
+    def tp_sum(a):
+        lane = a * T + tp
+        q, k = q_rows(lane), k_view(lane)[...]
+        for d in range(T - 1):
+            q = q + bq[d, a].astype(jnp.float32)
+            k = k + bk[d, a]
+        return q, k
+
+    far = []
+    for d in range(1, S):
+        s2 = lax.rem(st + d, S)
+        q, k = tp_sum(s2)
+        ck[d - 1] = k
+        cq[d - 1] = q.astype(jnp.bfloat16)
+        for kind, (src, dst) in enumerate(((ck, ek), (cq, eq))):
+            copy = pltpu.make_async_remote_copy(
+                src_ref=src.at[d - 1], dst_ref=dst.at[d - 1],
+                send_sem=s_send.at[kind, d - 1], recv_sem=s_recv.at[kind, d - 1],
+                device_id={"stg": s2}, device_id_type=MESH,
+            )
+            copy.start()
+            far.append(copy)
+    q, k = tp_sum(st)
+    for copy in far:
+        copy.wait_recv()
+    for d in range(S - 1):
+        q = q + eq[d].astype(jnp.float32)
+        k = k + ek[d]
+    cols = (st * T + tp) * kw + lax.broadcasted_iota(jnp.int32, k.shape, 0)
+    latent = cols < KVL
+    ss[0:1, :] = jnp.sum(q * q, axis=0, keepdims=True)
+    ss[1:2, :] = jnp.sum(jnp.where(latent, k * k, 0.0), axis=0, keepdims=True)
+    small = []
+    for i, (a, b) in enumerate(lane_steps):
+        copy = pltpu.make_async_remote_copy(
+            src_ref=ss, dst_ref=ssin.at[i], send_sem=v_send.at[i], recv_sem=v_recv.at[i],
+            device_id=lane_at(a, b), device_id_type=MESH,
+        )
+        copy.start()
+        small.append(copy)
+    sq = ss[...]
+    for i, copy in enumerate(small):
+        copy.wait_recv()
+        sq = sq + ssin[i]
+    qn = q * lax.rsqrt(sq[0:1] / QL + norm_eps) * qg_ref[...]
+    q_out[...] = jnp.transpose(qn).astype(jnp.bfloat16)
+    kn = k * jnp.where(latent, lax.rsqrt(sq[1:2] / KVL + norm_eps) * kg_ref[...], 1.0)
+    even = lax.rem(lax.broadcasted_iota(jnp.int32, k.shape, 0), 2) == 0
+    partner = jnp.where(even, -pltpu.roll(kn, kw - 1, 0), pltpu.roll(kn, 1, 0))
+    k_out[...] = (kn * cos_ref[...] + partner * sin_ref[...]).astype(jnp.bfloat16)
+
+    for copy in copies + far + small:
+        copy.wait_send()
+    for s in range(D):
+        for c in range(K):
+            for way, j, there in sides(s):
+                @pl.when(there & can_send(way))
+                def _():
+                    z_copy(j, c, way, s == 0).wait_send()
+
+                if s > 0:
+                    @pl.when(there)
+                    def _():
+                        for d in range(1, G):
+                            y_copy(j, c, d).wait_send()
+
+
+def chunk_count(rows):
+    return next(k for k in (3, 2, 1) if rows % (16 * k) == 0)
+
+
+def fused_ok(hidden_x, proj_weight):
+    sizes = [lax.axis_size(n) for n in ("dec", "grp", "stg", "tp")]
+    lanes = sizes[2] * sizes[3]
+    return (
+        proj_weight.shape[1] % 16 == 0
+        and hidden_x.shape[0] % 128 == 0
+        and hidden_x.shape[1] % (128 * sizes[1]) == 0
+        and QL % (16 * lanes) == 0
+        and (KVL + ROPE) % (16 * lanes) == 0
+    )
+
+
+def fused_projection(hidden_x, proj_weight, q_gain, kv_gain, positions):
+    D, G, S, T = [lax.axis_size(n) for n in ("dec", "grp", "stg", "tp")]
+    L = S * T
+    rows, features = hidden_x.shape
+    C = proj_weight.shape[1]
+    K = chunk_count(C)
+    fg, qw, kw = features // G, QL // L, (KVL + ROPE) // L
+    lane = lax.axis_index(("stg", "tp"))
+    weight = jnp.transpose(proj_weight.reshape(G, fg, C), (0, 2, 1))
+    qg = lax.dynamic_slice_in_dim(q_gain, lane * qw, qw)[:, None]
+    gain_full = jnp.concatenate([kv_gain, jnp.ones((ROPE,), jnp.float32)])
+    kg = lax.dynamic_slice_in_dim(gain_full, lane * kw, kw)[:, None]
+    columns = lane * kw + jnp.arange(kw, dtype=jnp.int32)
+    is_rope = (columns >= KVL)[:, None]
+    pair_index = jnp.maximum(columns - KVL, 0) // 2
+    frequency = jnp.power(jnp.float32(10000.0), -(2 * pair_index).astype(jnp.float32) / ROPE)
+    angles = frequency[:, None] * positions[None, :]
+    cosine = jnp.where(is_rope, jnp.cos(angles), 1.0)
+    sine = jnp.where(is_rope, jnp.sin(angles), 0.0)
+    dma = pltpu.SemaphoreType.DMA
+    bf, f32 = jnp.bfloat16, jnp.float32
+    t1, s1, g1 = max(T - 1, 1), max(S - 1, 1), max(G - 1, 1)
+    q_out, k_out = pl.pallas_call(
+        functools.partial(proj_kernel, (D, G, S, T, K)),
+        out_shape=(
+            jax.ShapeDtypeStruct((rows, qw), bf),
+            jax.ShapeDtypeStruct((kw, rows), bf),
+        ),
+        in_specs=[pl.BlockSpec(memory_space=pltpu.VMEM)] * 6,
+        out_specs=(pl.BlockSpec(memory_space=pltpu.VMEM),) * 2,
+        scratch_shapes=[
+            pltpu.VMEM((D, G, C, fg), bf),
+            pltpu.VMEM((D * C, rows), f32),
+            pltpu.VMEM((t1, S, qw, rows), bf),
+            pltpu.VMEM((t1, S, qw, rows), bf),
+            pltpu.VMEM((t1, S, kw, rows), f32),
+            pltpu.VMEM((s1, qw, rows), bf),
+            pltpu.VMEM((s1, kw, rows), f32),
+            pltpu.VMEM((s1, qw, rows), bf),
+            pltpu.VMEM((s1, kw, rows), f32),
+            pltpu.VMEM((8, rows), f32),
+            pltpu.VMEM((max(L - 1, 1), 8, rows), f32),
+            dma((2, D, K)), dma((D, K)), dma((g1, D, K)), dma((g1, D, K)),
+            dma((2, t1, S)), dma((2, t1, S)), dma((2, s1)), dma((2, s1)),
+            dma((max(L - 1, 1),)), dma((max(L - 1, 1),)),
+        ],
+        compiler_params=pltpu.CompilerParams(
+            collective_id=0, has_side_effects=True, vmem_limit_bytes=48 * 1024 * 1024
+        ),
+    )(weight, hidden_x, qg, kg, cosine, sine)
+    return q_out, jnp.transpose(k_out)
+
+
 def body(
     hidden_x,
     proj_weight,
@@ -103,13 +387,6 @@
     dec_query,
     new_key,
 ):
-    projected = jnp.dot(
-        hidden_x,
-        lax.all_gather(proj_weight, "dec", axis=1, tiled=True),
-        preferred_element_type=jnp.float32,
-    )
-    query_part = projected[:, :QL]
-    kv_part = projected[:, QL:]
     tokens_here = hidden_x.shape[0]
     positions = (
         lax.axis_index("dec") * tokens_here + jnp.arange(tokens_here, dtype=jnp.int32)
@@ -120,18 +397,33 @@
     page_count = page_plan.shape[0]
     capacity = max(2, -(-page_count // owner_count))
     query_width = QL // lane_count
-    query_cols, kv_cols = (
-        lax.psum_scatter(query_part, ("stg", "tp"), scatter_dimension=1, tiled=True),
-        lax.psum_scatter(kv_part, ("stg", "tp"), scatter_dimension=1, tiled=True),
-    )
-    kv_width = kv_cols.shape[1]
-    col_start = lane_index * kv_width
-    columns = col_start + jnp.arange(kv_width, dtype=jnp.int32)
-    latent_part_sq = jnp.sum(jnp.where(columns[None, :] < KVL, kv_cols * kv_cols, 0.0), axis=1)
-    query_sq, latent_sq = lax.psum(
-        (jnp.sum(query_cols * query_cols, axis=1), latent_part_sq), ("stg", "tp")
-    )
-    kv_rows = kv_finish(kv_cols, col_start, latent_sq, kv_gain, positions)
+    if fused_ok(hidden_x, proj_weight):
+        q_latent, kv_rows = fused_projection(hidden_x, proj_weight, q_gain, kv_gain, positions)
+    else:
+        projected = jnp.dot(
+            hidden_x,
+            lax.all_gather(proj_weight, "dec", axis=1, tiled=True),
+            preferred_element_type=jnp.float32,
+        )
+        query_part = projected[:, :QL]
+        kv_part = projected[:, QL:]
+        query_cols, kv_cols = (
+            lax.psum_scatter(query_part, ("stg", "tp"), scatter_dimension=1, tiled=True),
+            lax.psum_scatter(kv_part, ("stg", "tp"), scatter_dimension=1, tiled=True),
+        )
+        kv_width = kv_cols.shape[1]
+        col_start = lane_index * kv_width
+        columns = col_start + jnp.arange(kv_width, dtype=jnp.int32)
+        latent_part_sq = jnp.sum(jnp.where(columns[None, :] < KVL, kv_cols * kv_cols, 0.0), axis=1)
+        query_sq, latent_sq = lax.psum(
+            (jnp.sum(query_cols * query_cols, axis=1), latent_part_sq), ("stg", "tp")
+        )
+        kv_rows = kv_finish(kv_cols, col_start, latent_sq, kv_gain, positions)
+        query_gain = lax.dynamic_slice_in_dim(q_gain, lane_index * query_width, query_width)
+        q_latent = (
+            query_cols * lax.rsqrt(query_sq / QL + norm_eps)[:, None] * query_gain[None, :]
+        ).astype(jnp.bfloat16)
+    kv_width = kv_rows.shape[1]
     kv_pages = kv_rows.reshape(page_count, PAGE, kv_width)
     send_pages, send_labels = pack_pages(kv_pages, page_plan, owner_count, capacity)
     got_slices, got_labels = (
@@ -139,10 +431,6 @@
         lax.all_to_all(send_labels, "dec", split_axis=0, concat_axis=0, tiled=True),
     )
     got_pages = lax.all_gather(got_slices, ("stg", "tp"), axis=3, tiled=True)
-    query_gain = lax.dynamic_slice_in_dim(q_gain, lane_index * query_width, query_width)
-    q_latent = (
-        query_cols * lax.rsqrt(query_sq / QL + norm_eps)[:, None] * query_gain[None, :]
-    ).astype(jnp.bfloat16)
     cache = place_pages(old_cache, got_pages, got_labels)
     slot_table = block_table[0]
     request_count = slot_table.shape[0]

time: 304 us -> 189 us (0.62)
  waiting for transfers between devices: 195 us -> 9.63 us
  Pallas kernels: 0 us -> 93.7 us
  local copies, waits for them, and re-layouts: 20.2 us -> 12.8 us
  blocking collectives: 43.7 us -> 36.5 us
  matrix products: 8.18 us -> 1.78 us
  other arithmetic: 13.6 us -> 9.92 us
    all_gather x1 -> x0, waiting for transfers between devices: 141 us -> none  [body(): lax.all_gather(proj_weight, 'dec', axis=1, tiled=True)]
    pallas_call x0 -> x1, Pallas kernels: none -> 93.7 us  [fused_projection(): pl.pallas_call(functools.partial(proj_kernel, (D, G, S, T, K)), out_shape...]
    reduce_scatter x2 -> x0, waiting for transfers between devices: 41.6 us -> none  [the longest x1 34.3 us: body(): lax.psum_scatter(query_part, ('stg', 'tp'), scatter_dimension=1, tiled=True)]
    dot_general x1 -> x0, matrix products: 6.4 us -> none  [body(): jnp.dot(hidden_x, lax.all_gather(proj_weight, 'dec', axis=1, tiled=True),...]
    psum x1 -> x0, blocking collectives: 5.75 us -> none  [body(): lax.psum((jnp.sum(query_cols * query_cols, axis=1), latent_part_sq), ('st...]
    all_to_all x1, waiting for transfers between devices: 4.79 us -> 0.01 us  [body(): lax.all_to_all(send_labels, 'dec', split_axis=0, concat_axis=0, tiled=True)]
    slice x2 -> x0, local copies, waits for them, and re-layouts: 4.25 us -> none  [the longest x1 3.27 us: body(): query_part = projected[:, :QL]]
    unnamed x21 -> x9, local copies, waits for them, and re-layouts: 3.91 us -> 0.74 us
  transfers between devices with their start and end apart: 6 -> 3, of which waited for: 6 -> 2; matrix products, arithmetic and copies ran while one was open for 3% -> 4% of each run, Pallas kernels for 0% -> 50%
where the time goes in v1:
time: 189 us
  Pallas kernels  93.7 us (50%)
  blocking collectives  36.5 us (19%)
  between operations  14.3 us (8%)
  local copies, waits for them, and re-layouts  12.8 us (7%)
  starting transfers between devices  9.98 us (5%)
  other arithmetic  9.92 us (5%)
  waiting for transfers between devices  9.63 us (5%)
    pallas_call x1, Pallas kernels, fused_projection(): pl.pallas_call(functools.partial(proj_kernel, (D, G, S, T, K)), out_shape...  93.7 us
    all_gather x2, blocking collectives, combined_all(): gathered = jax.tree.map(lambda a: lax.all_gather(a, axis), part)  24.3 us
    all_gather x1, blocking collectives, body(): got_pages = lax.all_gather(got_slices, ('stg', 'tp'), axis=3, tiled=True)  12.2 us
    all_to_all x1, waiting for transfers between devices, body(): lax.all_to_all(send_pages, 'dec', split_axis=0, concat_axis=0, tiled=True)  7.03 us
    all_to_all x1, starting transfers between devices, body(): lax.all_to_all(send_labels, 'dec', split_axis=0, concat_axis=0, tiled=True)  6.35 us
  transfers between devices with their start and end apart: 3, of which 2 were waited for; matrix products, arithmetic and copies ran while one was open for 4% of the time, Pallas kernels for 50%

profile of v1, /device:TPU:0, one launch (start us, length us, event | category | flops | bytes accessed | tf_op | source)
XLA Modules:
  0.0 188.6 jit_solution(6515505072815438881)
XLA Ops:
  10.6 6.3 %all-to-all-start = ((bf16[4,1,3]{2,1,0:T(2,128)(2,1)}), bf16[4,1,3]{2,1,0:T(2,128)(2,1)S(1)}, u32[]{:S(2)}, u32[]{:S(2)}) async-start(bf16[4,1,3]{2,1,0:T(2,128)(2,1)} %copy.29), calls=%async_computation | async-start | bytes 4096 | tf_op jit(solution)/shard_map/all_to_all | solution.py:431
  17.1 0.8 reshape_squeeze.6
  19.5 0.8 dynamic_slice.47
  20.4 1.8 copy.41
  22.1 0.9 fusion.8
  23.0 93.7 %shard_map.113 = (bf16[384,384]{1,0:T(8,128)(2,1)S(1)}, bf16[144,384]{1,0:T(8,128)(2,1)S(1)}) custom-call(bf16[2,528,896]{2,1,0:T(8,128)(2,1)S(1)} %bitcast.70, bf16[384,1792]{1,0:T(8,128)(2,1)S(1)} %copy-done.1, f32[384,1]{1,0:T(8,128)S(1)} %broadcast_in_dim.181.qg_ref, f32[144,1]{1,0:T(8,128)S(1)} %copy.28.kg_ref, ...), custom_call_target="tpu_custom_call" | custom-call | tf_op jit(solution)/shard_map/pallas_call | solution.py:347
  117.7 0.8 select_select_fusion.1
  118.5 3.6 %all-to-all-start.1 = ((bf16[4,3,32,144]{3,2,1,0:T(8,128)(2,1)}), bf16[4,3,32,144]{3,2,1,0:T(8,128)(2,1)S(1)}, u32[]{:S(2)}, u32[]{:S(2)}) async-start(bf16[4,3,32,144]{3,2,1,0:T(8,128)(2,1)} %select_select_fusion.1), calls=%async_computation.1 | async-start | bytes 393216 | tf_op jit(solution)/shard_map/all_to_all | solution.py:430
  122.5 7.0 %all-to-all-done.1 = bf16[4,3,32,144]{3,2,1,0:T(8,128)(2,1)S(1)} async-done(((bf16[4,3,32,144]{3,2,1,0:T(8,128)(2,1)}), bf16[4,3,32,144]{3,2,1,0:T(8,128)(2,1)S(1)}, u32[]{:S(2)}, u32[]{:S(2)}) %all-to-all-start.1) | async-done | bytes 110624 | tf_op jit(solution)/shard_map/all_to_all | solution.py:430
  129.8 12.2 %all_gather.21 = bf16[4,3,32,576]{2,0,1,3:T(4,128)(2,1)S(1)} all-gather(bf16[4,3,32,144]{2,0,1,3:T(4,128)(2,1)S(1)} %copy.31), channel_id=1, replica_groups=mesh['grp'=2,'dec'=4,'stg'=2,'tp'=2] {'stg','tp'}, dimensions={3}, use_global_device_ids=true | all-gather | bytes 552960 | tf_op jit(solution)/shard_map/all_gather | solution.py:433
  142.0 1.6 copy.32
  143.5 0.8 gather_fusion.2
  144.3 1.6 select_select_fusion
  145.9 0.8 gather_fusion.3
  147.6 1.1 fusion.5
  149.0 12.0 %all-gather.4 = f32[4,4,32]{2,1,0:T(4,128)S(1)} all-gather(f32[1,4,32]{2,1,0:T(4,128)S(1)} %bitcast.79), channel_id=3, replica_groups=mesh['grp'=2,'dec'=4,'stg'=2,'tp'=2] {'dec'}, dimensions={0}, use_global_device_ids=true | all-gather | bytes 2560 | tf_op jit(solution)/shard_map/all_gather | solution.py:21
  161.0 12.3 %all-gather.3 = f32[4,4,32]{2,1,0:T(4,128)S(1)} all-gather(f32[1,4,32]{2,1,0:T(4,128)S(1)} %bitcast.78), channel_id=2, replica_groups=mesh['grp'=2,'dec'=4,'stg'=2,'tp'=2] {'dec'}, dimensions={0}, use_global_device_ids=true | all-gather | bytes 2560 | tf_op jit(solution)/shard_map/all_gather | solution.py:21
  173.3 2.6 %all-gather.7.cloned.1.call-done = f32[16,32,512]{2,1,0:T(8,128)} async-done(((f32[4,32,512]{2,1,0:T(8,128)}), f32[16,32,512]{2,1,0:T(8,128)}) %all-gather.7.cloned.1.call-update) | async-done | bytes 1048592 | tf_op jit(solution)/shard_map/all_gather | solution.py:21
  175.9 1.0 slice.35
  176.9 3.4 %while.19 = (s32[]{:T(128)}, f32[4,32]{1,0:T(4,128)S(1)}, f32[4,32]{1,0:T(4,128)S(1)}, f32[4,32,512]{2,1,0:T(8,128)S(1)}, f32[4,4,32]{2,1,0:T(4,128)S(1)}, /*ind...) while((s32[]{:T(128)}, f32[4,32]{1,0:T(4,128)S(1)}, ...), condition=%wide.region_8.9_spmd, body=%wide.region_7.8_spmd.sunk | while | flops 197381 | bytes 791703 | solution.py:26
  176.9 1.1 fusion.37
  178.0 1.1 fusion.37
  179.2 1.1 fusion.37
  180.3 0.8 divide_convert_fusion
  (61 shorter events, 8.8 us)
Async XLA Ops:
  7.2 139.8 %copy-start = (bf16[4,32,576]{2,1,0:T(8,128)(2,1)S(1)}, bf16[4,32,576]{2,1,0:T(8,128)(2,1)}, u32[]{:S(2)}) copy-start(bf16[4,32,576]{2,1,0:T(8,128)(2,1)} %param.20) | copy-start | bytes 442372
  10.6 107.9 %all-to-all-start = ((bf16[4,1,3]{2,1,0:T(2,128)(2,1)}), bf16[4,1,3]{2,1,0:T(2,128)(2,1)S(1)}, u32[]{:S(2)}, u32[]{:S(2)}) async-start(bf16[4,1,3]{2,1,0:T(2,128)(2,1)} %copy.29), calls=%async_computation | async-start | bytes 4096 | tf_op jit(solution)/shard_map/all_to_all | solution.py:431
  20.3 2.7 %copy-start.1 = (bf16[384,1792]{1,0:T(8,128)(2,1)S(1)}, bf16[384,1792]{1,0:T(8,128)(2,1)}, u32[]{:S(2)}) copy-start(bf16[384,1792]{1,0:T(8,128)(2,1)} %x_ref.1) | copy-start | bytes 4128772
  23.0 94.6 %copy-start.3 = (s32[4,1]{0,1:T(1,128)S(1)}, s32[4,1]{0,1:T(1,128)}, u32[]{:S(2)}) copy-start(s32[4,1]{0,1:T(1,128)} %param.19) | copy-start | bytes 52
  118.5 11.0 %all-to-all-start.1 = ((bf16[4,3,32,144]{3,2,1,0:T(8,128)(2,1)}), bf16[4,3,32,144]{3,2,1,0:T(8,128)(2,1)S(1)}, u32[]{:S(2)}, u32[]{:S(2)}) async-start(bf16[4,3,32,144]{3,2,1,0:T(8,128)(2,1)} %select_select_fusion.1), calls=%async_computation.1 | async-start | bytes 393216 | tf_op jit(solution)/shard_map/all_to_all | solution.py:430
  122.1 53.8 %all-gather.7.cloned.1.call-start = ((), (), s32[]{:S(2)}) async-start(), calls=%async_computation.2 | async-start | bytes 1310720 | tf_op jit(solution)/shard_map/all_gather | solution.py:21
  147.0 1.7 copy-start.2
Sparse Core Ops, SparseCore 0:
  148.8 27.0 all-gather.6

commit v2 on v0

--- a/solution.py
+++ b/solution.py
@@ -1,6 +1,10 @@
+import functools
+
 import jax
 import jax.numpy as jnp
 from jax import lax
+from jax.experimental import pallas as pl
+from jax.experimental.pallas import tpu as pltpu
 from jax.sharding import PartitionSpec as P
 
 QL = 1536
@@ -91,6 +95,550 @@
     )
 
 
+MESH = pl.DeviceIdType.MESH
+
+
+def fused_kernel(
+    dims, w_ref, x_ref, qg_ref, kg_ref, cos_ref, sin_ref, src_ref, bt_ref, lens_ref,
+    plan_ref, want_ref, old_ref, dq_ref, nk_ref, q_out, a_out,
+    wbuf, pt, aq, bq, cq, eq, ss, ssin, kvp, bk, ck, ek, kvl, sendp, got, plans,
+    found, found_s, kbuf, part, parts, selfs, newk, fin,
+    local_sem, zsem, zrecv, ysem, yrecv, t_send, t_recv, s_send, s_recv, v_send, v_recv,
+    tk_send, tk_recv, sk_send, sk_recv, l_send, l_recv, pl_send, pl_recv, pg_send, pg_recv,
+    c_send, c_recv, f_send, f_recv,
+):
+    D, G, S, T, K = dims
+    C, fg = w_ref.shape[1], w_ref.shape[2]
+    qw = qg_ref.shape[0]
+    rows, kvw = kvp.shape
+    lane_rows = rows // (S * T)
+    chunk_rows = C // K
+    cap = sendp.shape[1]
+    requests, spans = kbuf.shape[0], kbuf.shape[1]
+    table_width = spans // PAGE
+    fold = part.shape[0] // D
+    me, g = lax.axis_index("dec"), lax.axis_index("grp")
+    st, tp = lax.axis_index("stg"), lax.axis_index("tp")
+    lane = st * T + tp
+    lane_steps = [(a, b) for a in range(S) for b in range(T) if a or b]
+
+    def lane_at(a, b):
+        return {"stg": lax.rem(st + a, S), "tp": lax.rem(tp + b, T)}
+
+    def remote(src, dst, send, recv, target):
+        return pltpu.make_async_remote_copy(
+            src_ref=src, dst_ref=dst, send_sem=send, recv_sem=recv,
+            device_id=target, device_id_type=MESH,
+        )
+
+    own = pltpu.make_async_copy(
+        w_ref, wbuf.at[:, pl.ds(pl.multiple_of(me * C, 16), C)], local_sem.at[0]
+    )
+    own.start()
+    barrier = pltpu.get_barrier_semaphore()
+    greeted = [{"dec": lax.rem(me + d, D)} for d in range(1, D)]
+    greeted += [{"grp": lax.rem(g + d, G)} for d in range(1, G)]
+    greeted += [lane_at(a, b) for a, b in lane_steps]
+    for target in greeted:
+        pl.semaphore_signal(barrier, inc=1, device_id=target, device_id_type=MESH)
+    pl.semaphore_wait(barrier, len(greeted))
+
+    def chunk(j, half, c):
+        start = pl.multiple_of(j * C + c * chunk_rows, 16)
+        return wbuf.at[half, pl.ds(start, chunk_rows)]
+
+    def z_copy(j, c, way, mine):
+        src = w_ref.at[g, pl.ds(c * chunk_rows, chunk_rows)] if mine else chunk(j, g, c)
+        to = me + 1 if way == 0 else me - 1
+        return remote(src, chunk(j, g, c), zsem.at[way, j, c], zrecv.at[j, c], {"dec": to})
+
+    def y_copy(j, c, d):
+        return remote(
+            chunk(j, g, c), chunk(j, g, c), ysem.at[d - 1, j, c], yrecv.at[d - 1, j, c],
+            {"grp": lax.rem(g + d, G)},
+        )
+
+    def y_arrive(j, c, d):
+        half = lax.rem(g + G - d, G)
+        return remote(
+            chunk(j, half, c), chunk(j, half, c), ysem.at[d - 1, j, c],
+            yrecv.at[d - 1, j, c], {"grp": half},
+        )
+
+    def own_left(turn):
+        @pl.when((me > 0) & (me == D - 1 - turn))
+        def _():
+            for c in reversed(range(K)):
+                z_copy(me, c, 1, True).start()
+
+    plan_copies = []
+    plans[me] = plan_ref[...]
+    for d in range(1, D):
+        copy = remote(
+            plan_ref, plans.at[me], pl_send.at[d - 1], pl_recv.at[d - 1],
+            {"dec": lax.rem(me + d, D)},
+        )
+        copy.start()
+        plan_copies.append(copy)
+    own_left(0)
+
+    @pl.when(me < D - 1)
+    def _():
+        for c in reversed(range(K)):
+            z_copy(me, c, 0, True).start()
+
+    own.wait()
+
+    def project(j):
+        @pl.when(j * C < QL)
+        def _():
+            block = pl.ds(pl.multiple_of(j * C, 16), C)
+            total = None
+            for half in range(G):
+                term = lax.dot_general(
+                    wbuf[half, block, :], x_ref[:, half * fg : (half + 1) * fg],
+                    (((1,), (1,)), ((), ())), preferred_element_type=jnp.float32,
+                )
+                total = term if total is None else total + term
+            pt[block, :] = total
+
+    project(me)
+
+    def is_kv(j, c):
+        return j * C + (c + 1) * chunk_rows > QL
+
+    def finish_block(j, there):
+        for c in range(K):
+            @pl.when(there & jnp.logical_not(is_kv(j, c)))
+            def _():
+                for d in range(1, G):
+                    y_arrive(j, c, d).wait_recv()
+
+        @pl.when(there)
+        def _():
+            project(j)
+
+    def relay(n):
+        turn, c = n // K, K - 1 - n % K
+        jr, jl = me - 1 - turn, D - 1 - turn
+        if n % K == 0 and turn > 0:
+            own_left(turn)
+
+        @pl.when(jl > me)
+        def _():
+            z_copy(jl, c, 1, False).wait_recv()
+
+            @pl.when(me > 0)
+            def _():
+                z_copy(jl, c, 1, False).start()
+            for d in range(1, G):
+                y_copy(jl, c, d).start()
+
+        @pl.when(jr >= 0)
+        def _():
+            z_copy(jr, c, 0, False).wait_recv()
+
+            @pl.when(me < D - 1)
+            def _():
+                z_copy(jr, c, 0, False).start()
+
+            @pl.when(me == D - 1)
+            def _():
+                for d in range(1, G):
+                    y_copy(jr, c, d).start()
+        if turn > 0:
+            @pl.when((me < D - 1) & (jr + 1 >= 0))
+            def _():
+                for d in range(1, G):
+                    y_copy(jr + 1, c, d).start()
+
+    tk, sk, lk, pg, cc, ff = [], [], [], [], [], []
+
+    def k_rows(at):
+        return kvp.at[pl.ds(pl.multiple_of(at * lane_rows, 16), lane_rows)]
+
+    def kv_project():
+        for j in range(D):
+            for c in range(K):
+                if is_kv(j, c):
+                    @pl.when(me != j)
+                    def _():
+                        for d in range(1, G):
+                            y_arrive(j, c, d).wait_recv()
+        total = None
+        for half in range(G):
+            term = lax.dot_general(
+                x_ref[:, half * fg : (half + 1) * fg], wbuf[half, QL:, :],
+                (((1,), (1,)), ((), ())), preferred_element_type=jnp.float32,
+            )
+            total = term if total is None else total + term
+        kvp[...] = total
+        for d in range(1, T):
+            t2 = lax.rem(tp + d, T)
+            for a in range(S):
+                copy = remote(
+                    k_rows(a * T + t2), bk.at[d - 1, a], tk_send.at[d - 1, a],
+                    tk_recv.at[d - 1, a], {"tp": t2},
+                )
+                copy.start()
+                tk.append(copy)
+
+    def kv_tp(a):
+        k = k_rows(a * T + tp)[...]
+        for d in range(T - 1):
+            k = k + bk[d, a]
+        return k
+
+    def kv_across():
+        for copy in tk:
+            copy.wait_recv()
+        for d in range(1, S):
+            s2 = lax.rem(st + d, S)
+            ck[d - 1] = kv_tp(s2)
+            copy = remote(
+                ck.at[d - 1], ek.at[d - 1], sk_send.at[d - 1], sk_recv.at[d - 1], {"stg": s2}
+            )
+            copy.start()
+            sk.append(copy)
+
+    def kv_norm():
+        for copy in sk:
+            copy.wait_recv()
+        k = kv_tp(st)
+        for d in range(S - 1):
+            k = k + ek[d]
+        lat, tail = k[:, :KVL], k[:, KVL:]
+        square = jnp.sum(lat * lat, axis=1, keepdims=True)
+        lat = lat * (lax.rsqrt(square / KVL + norm_eps) * kg_ref[...])
+        to = lax.broadcasted_iota(jnp.int32, (ROPE, ROPE), 1)
+        at = lax.broadcasted_iota(jnp.int32, (ROPE, ROPE), 0)
+        even = lax.rem(to, 2) == 0
+        swap = jnp.where(even & (at == to + 1), -1.0, 0.0)
+        swap = jnp.where(jnp.logical_not(even) & (at == to - 1), 1.0, swap)
+        partner = jnp.dot(
+            tail, swap, preferred_element_type=jnp.float32, precision=lax.Precision.HIGHEST
+        )
+        tail = tail * cos_ref[...] + partner * sin_ref[...]
+        pages = lane_rows // PAGE
+        mine = pl.ds(lane * pages, pages)
+        kvl[mine, :, :KVL] = lat.astype(jnp.bfloat16).reshape(pages, PAGE, KVL)
+        kvl[mine, :, KVL:] = tail.astype(jnp.bfloat16).reshape(pages, PAGE, ROPE)
+        for i, (a, b) in enumerate(lane_steps):
+            copy = remote(
+                kvl.at[mine], kvl.at[mine], l_send.at[i], l_recv.at[i], lane_at(a, b)
+            )
+            copy.start()
+            lk.append(copy)
+        for copy in plan_copies:
+            copy.wait_recv()
+        total = jnp.zeros(want_ref.shape, jnp.int32)
+        for d in range(D):
+            keys, ranks = plans[d, 0:1, :], plans[d, 1:2, :]
+            total = total + jnp.where(keys == want_ref[...], d * cap + ranks + 1, 0)
+        found[...] = jnp.broadcast_to(jnp.sum(total, axis=1, keepdims=True), found.shape)
+        copy = pltpu.make_async_copy(found, found_s, local_sem.at[1])
+        copy.start()
+        copy.wait()
+
+    def send_pages():
+        for copy in lk:
+            copy.wait_recv()
+        for o in range(D):
+            for r in range(cap):
+                sendp[o, r] = kvl[src_ref[o * cap + r]]
+        for d in range(1, D):
+            to = lax.rem(me + d, D)
+            copy = remote(
+                sendp.at[to], got.at[me], pg_send.at[d - 1], pg_recv.at[d - 1], {"dec": to}
+            )
+            copy.start()
+            pg.append(copy)
+        got[me] = sendp[me]
+        for r in range(requests):
+            query = dq_ref[r].astype(jnp.float32)
+            row = nk_ref[pl.ds(r, 1), :].astype(jnp.float32)
+            score = jnp.sum(query * row, axis=1, keepdims=True) * softmax_scale
+            heads = query.shape[0]
+            selfs[r * heads : (r + 1) * heads, :] = jnp.broadcast_to(score, (heads, 128))
+            newk[r * heads : (r + 1) * heads, :] = jnp.broadcast_to(row[:, :KVL], (heads, KVL))
+
+    def attend():
+        for copy in pg:
+            copy.wait_recv()
+        for r in range(requests):
+            for j in range(table_width):
+                place = r * table_width + j
+                index = found_s[place, 0]
+                came = jnp.clip(index - 1, 0, D * cap - 1)
+                fresh = got[came // cap, lax.rem(came, cap)].astype(jnp.float32)
+                stale = old_ref[bt_ref[place]].astype(jnp.float32)
+                page = jnp.where(jnp.full(fresh.shape, index, jnp.int32) > 0, fresh, stale)
+                kbuf[r, j * PAGE : (j + 1) * PAGE, :] = page.astype(jnp.bfloat16)
+        for r in range(requests):
+            scores = lax.dot_general(
+                dq_ref[r], kbuf[r], (((1,), (1,)), ((), ())), preferred_element_type=jnp.float32
+            ) * softmax_scale
+            live = lax.broadcasted_iota(jnp.int32, scores.shape, 1) < lens_ref[r]
+            scores = jnp.where(live, scores, -1e30)
+            peak = jnp.max(scores, axis=1, keepdims=True)
+            weight = jnp.where(live, jnp.exp(scores - peak), 0.0)
+            total = jnp.sum(weight, axis=1, keepdims=True)
+            heads = scores.shape[0]
+            at = pl.ds(r * heads, heads)
+            part[at, :KVL] = jnp.dot(
+                weight.astype(jnp.bfloat16), kbuf[r, :, :KVL], preferred_element_type=jnp.float32
+            )
+            column = lax.broadcasted_iota(jnp.int32, (heads, 128), 1)
+            part[at, KVL:] = jnp.where(column < 64, peak, total)
+        for d in range(1, D):
+            to = lax.rem(me + d, D)
+            copy = remote(
+                part.at[pl.ds(pl.multiple_of(to * fold, 8), fold)], parts.at[d - 1],
+                c_send.at[d - 1], c_recv.at[d - 1], {"dec": to},
+            )
+            copy.start()
+            cc.append(copy)
+
+    def combine():
+        for copy in cc:
+            copy.wait_recv()
+        mine = pl.ds(pl.multiple_of(me * fold, 8), fold)
+        shares = [part[mine, :]] + [parts[d] for d in range(D - 1)]
+        own_score = selfs[mine, 0:1]
+        top = own_score
+        for share in shares:
+            top = jnp.maximum(top, share[:, KVL : KVL + 1])
+        own_weight = jnp.exp(own_score - top)
+        numer, denom = own_weight * newk[mine, :], own_weight
+        for share in shares:
+            factor = jnp.exp(share[:, KVL : KVL + 1] - top)
+            numer = numer + factor * share[:, :KVL]
+            denom = denom + factor * share[:, KVL + 64 : KVL + 65]
+        fin[me] = (numer / denom).astype(jnp.bfloat16)
+        for d in range(1, D):
+            copy = remote(
+                fin.at[me], fin.at[me], f_send.at[d - 1], f_recv.at[d - 1],
+                {"dec": lax.rem(me + d, D)},
+            )
+            copy.start()
+            ff.append(copy)
+
+    items = K * (D - 1)
+    kv_items = -(-kvw // chunk_rows)
+    stages = [kv_project, kv_across, kv_norm, send_pages, attend, combine]
+    first = min(kv_items + 3, items - 1)
+    gaps = (0, 2, 6, 9, 13, 17)
+    due = {}
+    for gap, stage in zip(gaps, stages):
+        due.setdefault(min(first + gap, items - 1), []).append(stage)
+    for n in range(items):
+        relay(n)
+        if n > first and n % K == (first + 1) % K:
+            turn = n // K - 1
+            finish_block(me - 1 - turn, (me - 1 - turn >= 0) & (me == D - 1))
+            if turn > 0:
+                finish_block(me - turn, (me - turn >= 0) & (me < D - 1))
+            finish_block(jnp.int32(D - 1 - turn), D - 1 - turn > me)
+        for stage in due.get(n, ()):
+            stage()
+    turn = D - 2
+    finish_block(me - 1 - turn, (me - 1 - turn >= 0) & (me == D - 1))
+    finish_block(me - turn, (me - turn >= 0) & (me < D - 1))
+    finish_block(jnp.int32(D - 1 - turn), D - 1 - turn > me)
+
+    def q_rows(at):
+        return pt[pl.ds(pl.multiple_of(at * qw, 16), qw), :]
+
+    near = []
+    for a in range(S):
+        for d in range(1, T):
+            t2 = lax.rem(tp + d, T)
+            aq[d - 1, a] = q_rows(a * T + t2).astype(jnp.bfloat16)
+            copy = remote(
+                aq.at[d - 1, a], bq.at[d - 1, a], t_send.at[d - 1, a], t_recv.at[d - 1, a],
+                {"tp": t2},
+            )
+            copy.start()
+            near.append(copy)
+    for copy in near:
+        copy.wait_recv()
+
+    def q_tp(a):
+        q = q_rows(a * T + tp)
+        for d in range(T - 1):
+            q = q + bq[d, a].astype(jnp.float32)
+        return q
+
+    far = []
+    for d in range(1, S):
+        s2 = lax.rem(st + d, S)
+        cq[d - 1] = q_tp(s2).astype(jnp.bfloat16)
+        copy = remote(
+            cq.at[d - 1], eq.at[d - 1], s_send.at[d - 1], s_recv.at[d - 1], {"stg": s2}
+        )
+        copy.start()
+        far.append(copy)
+    q = q_tp(st)
+    for copy in ff:
+        copy.wait_recv()
+    for e in range(D):
+        a_out[e * fold : (e + 1) * fold, :] = fin[e]
+    for copy in far:
+        copy.wait_recv()
+    for d in range(S - 1):
+        q = q + eq[d].astype(jnp.float32)
+    ss[...] = jnp.broadcast_to(jnp.sum(q * q, axis=0, keepdims=True), ss.shape)
+    small = []
+    for i, (a, b) in enumerate(lane_steps):
+        copy = remote(ss, ssin.at[i], v_send.at[i], v_recv.at[i], lane_at(a, b))
+        copy.start()
+        small.append(copy)
+    square = ss[...]
+    for i, copy in enumerate(small):
+        copy.wait_recv()
+        square = square + ssin[i]
+    q = q * lax.rsqrt(square[0:1] / QL + norm_eps) * qg_ref[...]
+    q_out[...] = jnp.transpose(q).astype(jnp.bfloat16)
+
+    for copy in plan_copies + tk + sk + lk + pg + cc + ff + near + far + small:
+        copy.wait_send()
+    for c in range(K):
+        @pl.when(me > 0)
+        def _():
+            z_copy(me, c, 1, True).wait_send()
+
+        @pl.when(me < D - 1)
+        def _():
+            z_copy(me, c, 0, True).wait_send()
+        for j in range(D):
+            @pl.when((j > me) & (me > 0))
+            def _():
+                z_copy(j, c, 1, False).wait_send()
+
+            @pl.when((j < me) & (me < D - 1))
+            def _():
+                z_copy(j, c, 0, False).wait_send()
+
+            @pl.when(j != me)
+            def _():
+                for d in range(1, G):
+                    y_copy(j, c, d).wait_send()
+
+
+def chunk_count(rows):
+    return next((k for k in (11, 3, 2) if rows % (16 * k) == 0), 1)
+
+
+def fused_ok(hidden_x, proj_weight, dec_query, page_plan):
+    D, G, S, T = [lax.axis_size(n) for n in ("dec", "grp", "stg", "tp")]
+    lanes, columns = S * T, proj_weight.shape[1]
+    return (
+        D > 2
+        and chunk_count(columns) > 5
+        and columns % 16 == 0
+        and (D - 2) * columns <= QL
+        and hidden_x.shape[0] % 128 == 0
+        and hidden_x.shape[0] % (PAGE * lanes) == 0
+        and hidden_x.shape[1] % (128 * G) == 0
+        and QL % (16 * lanes) == 0
+        and dec_query.shape[1] % 16 == 0
+        and dec_query.shape[0] * dec_query.shape[1] % (16 * D) == 0
+        and page_plan.shape[0] <= 128
+    )
+
+
+def fused(
+    hidden_x, proj_weight, q_gain, kv_gain, old_cache, page_plan, block_table, split_lens,
+    dec_query, new_key,
+):
+    D, G, S, T = [lax.axis_size(n) for n in ("dec", "grp", "stg", "tp")]
+    L = S * T
+    rows, features = hidden_x.shape
+    C = proj_weight.shape[1]
+    K = chunk_count(C)
+    fg, qw, kvw = features // G, QL // L, KVL + ROPE
+    lane, me = lax.axis_index(("stg", "tp")), lax.axis_index("dec")
+    lane_rows = rows // L
+    weight = jnp.transpose(proj_weight.reshape(G, fg, C), (0, 2, 1))
+    qg = lax.dynamic_slice_in_dim(q_gain, lane * qw, qw)[:, None]
+    positions = (
+        me * rows + lane * lane_rows + jnp.arange(lane_rows, dtype=jnp.int32)
+    ).astype(jnp.float32)
+    pair_index = jnp.arange(ROPE, dtype=jnp.int32) // 2
+    frequency = jnp.power(jnp.float32(10000.0), -(2 * pair_index).astype(jnp.float32) / ROPE)
+    angles = positions[:, None] * frequency[None, :]
+    cosine, sine = jnp.cos(angles), jnp.sin(angles)
+
+    pages, slots = page_plan.shape[0], old_cache.shape[0]
+    cap = max(2, -(-pages // D))
+    owners = page_plan[:, 0]
+    page_ids = jnp.arange(pages, dtype=jnp.int32)
+    earlier = (owners[:, None] == owners[None, :]) & (page_ids[None, :] < page_ids[:, None])
+    ranking = jnp.sum(earlier.astype(jnp.int32), axis=1)
+    places = jnp.arange(D * cap, dtype=jnp.int32)
+    matches = (owners * cap + ranking)[None, :] == places[:, None]
+    source_ids = jnp.sum(jnp.where(matches, page_ids[None, :], 0), axis=1)
+    plan = jnp.stack([owners * slots + page_plan[:, 1], ranking])
+    plan = jnp.pad(plan, ((0, 6), (0, 128 - pages)), constant_values=-1)
+    table = block_table.reshape(-1)
+    want = jnp.broadcast_to((me * slots + table)[:, None], (table.shape[0], 128))
+    requests, heads = dec_query.shape[0], dec_query.shape[1]
+    width = block_table.shape[2]
+    fold = requests * heads // D
+    dma = pltpu.SemaphoreType.DMA
+    bf, f32, i32 = jnp.bfloat16, jnp.float32, jnp.int32
+    t1, s1, g1, l1, d1 = max(T - 1, 1), max(S - 1, 1), max(G - 1, 1), max(L - 1, 1), D - 1
+    vmem = pl.BlockSpec(memory_space=pltpu.VMEM)
+    smem = pl.BlockSpec(memory_space=pltpu.SMEM)
+    q_out, a_out = pl.pallas_call(
+        functools.partial(fused_kernel, (D, G, S, T, K)),
+        out_shape=(
+            jax.ShapeDtypeStruct((rows, qw), bf),
+            jax.ShapeDtypeStruct((requests * heads, KVL), bf),
+        ),
+        in_specs=[vmem] * 6 + [smem] * 3 + [vmem] * 5,
+        out_specs=(vmem, vmem),
+        scratch_shapes=[
+            pltpu.VMEM((G, D * C, fg), bf),
+            pltpu.VMEM((D * C, rows), f32),
+            pltpu.VMEM((t1, S, qw, rows), bf),
+            pltpu.VMEM((t1, S, qw, rows), bf),
+            pltpu.VMEM((s1, qw, rows), bf),
+            pltpu.VMEM((s1, qw, rows), bf),
+            pltpu.VMEM((8, rows), f32),
+            pltpu.VMEM((l1, 8, rows), f32),
+            pltpu.VMEM((rows, kvw), f32),
+            pltpu.VMEM((t1, S, lane_rows, kvw), f32),
+            pltpu.VMEM((s1, lane_rows, kvw), f32),
+            pltpu.VMEM((s1, lane_rows, kvw), f32),
+            pltpu.VMEM((pages, PAGE, kvw), bf),
+            pltpu.VMEM((D, cap, PAGE, kvw), bf),
+            pltpu.VMEM((D, cap, PAGE, kvw), bf),
+            pltpu.VMEM((D, 8, 128), i32),
+            pltpu.VMEM((table.shape[0], 128), i32),
+            pltpu.SMEM((table.shape[0], 128), i32),
+            pltpu.VMEM((requests, width * PAGE, kvw), bf),
+            pltpu.VMEM((requests * heads, KVL + 128), f32),
+            pltpu.VMEM((d1, fold, KVL + 128), f32),
+            pltpu.VMEM((requests * heads, 128), f32),
+            pltpu.VMEM((requests * heads, KVL), f32),
+            pltpu.VMEM((D, fold, KVL), bf),
+            dma((2,)), dma((2, D, K)), dma((D, K)), dma((g1, D, K)), dma((g1, D, K)),
+            dma((t1, S)), dma((t1, S)), dma((s1,)), dma((s1,)), dma((l1,)), dma((l1,)),
+            dma((t1, S)), dma((t1, S)), dma((s1,)), dma((s1,)), dma((l1,)), dma((l1,)),
+            dma((d1,)), dma((d1,)), dma((d1,)), dma((d1,)),
+            dma((d1,)), dma((d1,)), dma((d1,)), dma((d1,)),
+        ],
+        compiler_params=pltpu.CompilerParams(
+            collective_id=0, has_side_effects=True, vmem_limit_bytes=56 * 1024 * 1024
+        ),
+    )(
+        weight, hidden_x, qg, kv_gain[None, :], cosine, sine, source_ids, table,
+        split_lens[:, 0], plan, want, old_cache, dec_query, new_key,
+    )
+    return q_out, a_out.reshape(requests, heads, KVL)
+
+
 def body(
     hidden_x,
     proj_weight,
@@ -103,6 +651,11 @@
     dec_query,
     new_key,
 ):
+    if fused_ok(hidden_x, proj_weight, dec_query, page_plan):
+        return fused(
+            hidden_x, proj_weight, q_gain, kv_gain, old_cache, page_plan, block_table,
+            split_lens, dec_query, new_key,
+        )
     projected = jnp.dot(
         hidden_x,
         lax.all_gather(proj_weight, "dec", axis=1, tiled=True),

time: 304 us -> 130 us (0.43)
  waiting for transfers between devices: 195 us -> 0 us
  Pallas kernels: 0 us -> 116 us
  blocking collectives: 43.7 us -> 0 us
  between operations: 14 us -> 0.66 us
  other arithmetic: 13.6 us -> 3.17 us
  local copies, waits for them, and re-layouts: 20.2 us -> 9.82 us
  matrix products: 8.18 us -> 0 us
  starting transfers between devices: 8.14 us -> 0 us
    all_gather x2 -> x0, waiting for transfers between devices: 141 us -> none  [the longest x1 141 us: body(): lax.all_gather(proj_weight, 'dec', axis=1, tiled=True)]
    pallas_call x0 -> x1, Pallas kernels: none -> 116 us  [fused(): pl.pallas_call(functools.partial(fused_kernel, (D, G, S, T, K)), out_shap...]
    reduce_scatter x2 -> x0, waiting for transfers between devices: 41.6 us -> none  [the longest x1 34.3 us: body(): lax.psum_scatter(query_part, ('stg', 'tp'), scatter_dimension=1, tiled=True)]
    all_gather x3 -> x0, blocking collectives: 38 us -> none  [the longest x2 24.5 us: combined_all(): gathered = jax.tree.map(lambda a: lax.all_gather(a, axis), part)]
    all_to_all x2 -> x0, waiting for transfers between devices: 12 us -> none  [the longest x1 7.2 us: body(): lax.all_to_all(send_pages, 'dec', split_axis=0, concat_axis=0, tiled=True)]
    dot_general x4 -> x0, matrix products: 8.18 us -> none  [the longest x1 6.4 us: body(): jnp.dot(hidden_x, lax.all_gather(proj_weight, 'dec', axis=1, tiled=True),...]
    all_to_all x2 -> x0, starting transfers between devices: 8.02 us -> none  [the longest x1 4.79 us: body(): lax.all_to_all(send_pages, 'dec', split_axis=0, concat_axis=0, tiled=True)]
    psum x1 -> x0, blocking collectives: 5.75 us -> none  [body(): lax.psum((jnp.sum(query_cols * query_cols, axis=1), latent_part_sq), ('st...]
  transfers between devices with their start and end apart: 6 -> 0, of which waited for: 6 -> 0; matrix products, arithmetic and copies ran while one was open for 3% -> 0% of each run, Pallas kernels for 0% -> 0%
where the time goes in v2:
time: 130 us
  Pallas kernels  116 us (89%)
  local copies, waits for them, and re-layouts  9.82 us (8%)
  other arithmetic  3.17 us (2%)
    pallas_call x1, Pallas kernels, fused(): pl.pallas_call(functools.partial(fused_kernel, (D, G, S, T, K)), out_shap...  116 us
    unnamed x4, local copies, waits for them, and re-layouts  3.28 us
    reshape x1, local copies, waits for them, and re-layouts, fused(): weight = jnp.transpose(proj_weight.reshape(G, fg, C), (0, 2, 1))  2.95 us

profile of v2, /device:TPU:0, one launch (start us, length us, event | category | flops | bytes accessed | tf_op | source)
XLA Modules:
  0.0 130.0 jit_solution(6990294352910316693)
XLA Ops:
  0.7 0.8 reshape.74.bt_ref
  1.4 0.0 copy-start
  1.4 0.8 add_bitcast_fusion
  2.2 0.2 convert_reduce_fusion
  2.4 0.7 multiply_add_fusion
  3.1 0.6 select_reduce_fusion.src_ref
  3.7 0.8 dynamic_slice.3
  4.5 0.6 pad.4.plan_ref
  5.1 0.7 broadcast_in_dim.19.want_ref
  5.7 0.9 multiply_sine_fusion
  6.6 0.8 broadcast_in_dim.20.qg_ref
  7.4 3.0 %copy.18 = bf16[66,2,8,896]{3,2,0,1:T(8,128)(2,1)} copy(bf16[66,2,8,896]{3,2,1,0:T(8,128)(2,1)} %bitcast.18) | data formatting | bytes 3784704 | tf_op jit(solution)/shard_map/reshape | solution.py:562
  10.4 0.0 copy-done
  10.4 116.4 %shard_map.113 = (bf16[384,384]{1,0:T(8,128)(2,1)}, bf16[128,512]{1,0:T(8,128)(2,1)}) custom-call(bf16[2,528,896]{2,1,0:T(8,128)(2,1)} %bitcast.17, bf16[384,1792]{1,0:T(8,128)(2,1)} %x_ref.1, f32[384,1]{1,0:T(8,128)} %broadcast_in_dim.20.qg_ref, f32[1,512]{1,0:T(1,128)} %bitcast.20, f32[96,64]{1,0:T(8,128)} %get-tuple-element.9.cos_ref, ...), custom_call_target="tpu_custom_call" | custom-call | tf_op jit(solution)/shard_map/pallas_call | solution.py:593
  126.7 1.7 %copy.21 = bf16[384,384]{1,0:T(8,128)(2,1)} copy(bf16[384,384]{1,0:T(8,128)(2,1)} %get-tuple-element.12) | data formatting | bytes 589824
  128.4 1.6 %copy.22 = bf16[4,32,512]{2,1,0:T(8,128)(2,1)} copy(bf16[4,32,512]{2,1,0:T(8,128)(2,1)} %bitcast.19) | data formatting | bytes 262144
  (4 shorter events, 0.0 us)
Async XLA Ops:
  1.4 9.0 %copy-start = (s32[32]{0:T(128)}, s32[32]{0:T(128)S(1)}, u32[]{:S(2)}) copy-start(s32[32]{0:T(128)S(1)} %reshape.74.bt_ref) | copy-start | bytes 388

commit v3 on v2

--- a/solution.py
+++ b/solution.py
@@ -109,7 +109,7 @@
 ):
     D, G, S, T, K = dims
     C, fg = w_ref.shape[1], w_ref.shape[2]
-    qw = qg_ref.shape[0]
+    qw = q_out.shape[1]
     rows, kvw = kvp.shape
     lane_rows = rows // (S * T)
     chunk_rows = C // K
@@ -165,11 +165,12 @@
             yrecv.at[d - 1, j, c], {"grp": half},
         )
 
-    def own_left(turn):
+    def own_left(turn, c):
         @pl.when((me > 0) & (me == D - 1 - turn))
         def _():
-            for c in reversed(range(K)):
-                z_copy(me, c, 1, True).start()
+            if turn > 0 and c < K - 2:
+                z_copy(me, c + 2, 1, True).wait_send()
+            z_copy(me, c, 1, True).start()
 
     plan_copies = []
     plans[me] = plan_ref[...]
@@ -180,7 +181,8 @@
         )
         copy.start()
         plan_copies.append(copy)
-    own_left(0)
+    for c in reversed(range(K)):
+        own_left(0, c)
 
     @pl.when(me < D - 1)
     def _():
@@ -221,8 +223,8 @@
     def relay(n):
         turn, c = n // K, K - 1 - n % K
         jr, jl = me - 1 - turn, D - 1 - turn
-        if n % K == 0 and turn > 0:
-            own_left(turn)
+        if turn > 0:
+            own_left(turn, c)
 
         @pl.when(jl > me)
         def _():
@@ -450,7 +452,9 @@
         return pt[pl.ds(pl.multiple_of(at * qw, 16), qw), :]
 
     near = []
-    for a in range(S):
+    for i in range(1, S + 1):
+        a = lax.rem(st + i, S)
+        group = []
         for d in range(1, T):
             t2 = lax.rem(tp + d, T)
             aq[d - 1, a] = q_rows(a * T + t2).astype(jnp.bfloat16)
@@ -459,9 +463,8 @@
                 {"tp": t2},
             )
             copy.start()
-            near.append(copy)
-    for copy in near:
-        copy.wait_recv()
+            group.append(copy)
+        near.append(group)
 
     def q_tp(a):
         q = q_rows(a * T + tp)
@@ -472,12 +475,16 @@
     far = []
     for d in range(1, S):
         s2 = lax.rem(st + d, S)
+        for copy in near[d - 1]:
+            copy.wait_recv()
         cq[d - 1] = q_tp(s2).astype(jnp.bfloat16)
         copy = remote(
             cq.at[d - 1], eq.at[d - 1], s_send.at[d - 1], s_recv.at[d - 1], {"stg": s2}
         )
         copy.start()
         far.append(copy)
+    for copy in near[S - 1]:
+        copy.wait_recv()
     q = q_tp(st)
     for copy in ff:
         copy.wait_recv()
@@ -497,13 +504,14 @@
     for i, copy in enumerate(small):
         copy.wait_recv()
         square = square + ssin[i]
-    q = q * lax.rsqrt(square[0:1] / QL + norm_eps) * qg_ref[...]
-    q_out[...] = jnp.transpose(q).astype(jnp.bfloat16)
-
-    for copy in plan_copies + tk + sk + lk + pg + cc + ff + near + far + small:
+    q = jnp.transpose(q * lax.rsqrt(square[0:1] / QL + norm_eps))
+    gain = qg_ref[:, pl.ds(pl.multiple_of(lane * qw, 128), qw)]
+    q_out[...] = (q * gain).astype(jnp.bfloat16)
+
+    for copy in plan_copies + tk + sk + lk + pg + cc + ff + sum(near, []) + far + small:
         copy.wait_send()
     for c in range(K):
-        @pl.when(me > 0)
+        @pl.when((me > 0) if c < 2 else (me == D - 1))
         def _():
             z_copy(me, c, 1, True).wait_send()
 
@@ -540,7 +548,7 @@
         and hidden_x.shape[0] % 128 == 0
         and hidden_x.shape[0] % (PAGE * lanes) == 0
         and hidden_x.shape[1] % (128 * G) == 0
-        and QL % (16 * lanes) == 0
+        and QL % (128 * lanes) == 0
         and dec_query.shape[1] % 16 == 0
         and dec_query.shape[0] * dec_query.shape[1] % (16 * D) == 0
         and page_plan.shape[0] <= 128
@@ -560,7 +568,7 @@
     lane, me = lax.axis_index(("stg", "tp")), lax.axis_index("dec")
     lane_rows = rows // L
     weight = jnp.transpose(proj_weight.reshape(G, fg, C), (0, 2, 1))
-    qg = lax.dynamic_slice_in_dim(q_gain, lane * qw, qw)[:, None]
+    qg = q_gain[None, :]
     positions = (
         me * rows + lane * lane_rows + jnp.arange(lane_rows, dtype=jnp.int32)
     ).astype(jnp.float32)

time: 130 us -> 129 us (level)
  no operation moved by 1% of the time
where the time goes in v3:
time: 129 us
  Pallas kernels  115 us (89%)
  local copies, waits for them, and re-layouts  9.56 us (7%)
  other arithmetic  3.19 us (2%)
    pallas_call x1, Pallas kernels, fused(): pl.pallas_call(functools.partial(fused_kernel, (D, G, S, T, K)), out_shap...  115 us
    unnamed x4, local copies, waits for them, and re-layouts  3.28 us
    reshape x1, local copies, waits for them, and re-layouts, fused(): weight = jnp.transpose(proj_weight.reshape(G, fg, C), (0, 2, 1))  2.95 us

profile of v3, /device:TPU:0, one launch (start us, length us, event | category | flops | bytes accessed | tf_op | source)
XLA Modules:
  0.0 128.8 jit_solution(2076650262069116954)
XLA Ops:
  0.7 0.8 reshape.74.bt_ref
  1.4 0.0 copy-start
  1.4 0.8 add_bitcast_fusion
  2.2 0.2 convert_reduce_fusion
  2.4 0.7 multiply_add_fusion
  3.1 0.6 select_reduce_fusion.src_ref
  3.7 0.6 pad.4.plan_ref
  4.3 1.3 %broadcast_in_dim.16.qg_ref = f32[1,1536]{1,0:T(1,128)} reshape(f32[1536]{0:T(1024)} %param.12) | data formatting | bytes 12288 | tf_op jit(solution)/shard_map/broadcast_in_dim | solution.py:571
  5.6 0.7 broadcast_in_dim.19.want_ref
  6.3 0.9 multiply_sine_fusion
  7.2 3.0 %copy.16 = bf16[66,2,8,896]{3,2,0,1:T(8,128)(2,1)} copy(bf16[66,2,8,896]{3,2,1,0:T(8,128)(2,1)} %bitcast.18) | data formatting | bytes 3784704 | tf_op jit(solution)/shard_map/reshape | solution.py:570
  10.1 0.0 copy-done
  10.1 115.4 %shard_map.113 = (bf16[384,384]{1,0:T(8,128)(2,1)}, bf16[128,512]{1,0:T(8,128)(2,1)}) custom-call(bf16[2,528,896]{2,1,0:T(8,128)(2,1)} %bitcast.17, bf16[384,1792]{1,0:T(8,128)(2,1)} %x_ref.1, f32[1,1536]{1,0:T(1,128)} %broadcast_in_dim.16.qg_ref, f32[1,512]{1,0:T(1,128)} %bitcast.20, f32[96,64]{1,0:T(8,128)} %get-tuple-element.9.cos_ref, ...), custom_call_target="tpu_custom_call" | custom-call | tf_op jit(solution)/shard_map/pallas_call | solution.py:601
  125.5 1.7 %copy.19 = bf16[384,384]{1,0:T(8,128)(2,1)} copy(bf16[384,384]{1,0:T(8,128)(2,1)} %get-tuple-element.12) | data formatting | bytes 589824
  127.3 1.6 %copy.20 = bf16[4,32,512]{2,1,0:T(8,128)(2,1)} copy(bf16[4,32,512]{2,1,0:T(8,128)(2,1)} %bitcast.19) | data formatting | bytes 262144
  (4 shorter events, 0.0 us)
Async XLA Ops:
  1.4 8.7 %copy-start = (s32[32]{0:T(128)}, s32[32]{0:T(128)S(1)}, u32[]{:S(2)}) copy-start(s32[32]{0:T(128)S(1)} %reshape.74.bt_ref) | copy-start | bytes 388

commit v4 on v3

--- a/solution.py
+++ b/solution.py
@@ -427,9 +427,9 @@
 
     items = K * (D - 1)
     kv_items = -(-kvw // chunk_rows)
-    stages = [kv_project, kv_across, kv_norm, send_pages, attend, combine]
+    stages = [kv_project, kv_across, kv_norm, send_pages]
     first = min(kv_items + 3, items - 1)
-    gaps = (0, 2, 6, 9, 13, 17)
+    gaps = (0, 2, 6, 10)
     due = {}
     for gap, stage in zip(gaps, stages):
         due.setdefault(min(first + gap, items - 1), []).append(stage)
@@ -465,6 +465,7 @@
             copy.start()
             group.append(copy)
         near.append(group)
+    attend()
 
     def q_tp(a):
         q = q_rows(a * T + tp)
@@ -486,10 +487,7 @@
     for copy in near[S - 1]:
         copy.wait_recv()
     q = q_tp(st)
-    for copy in ff:
-        copy.wait_recv()
-    for e in range(D):
-        a_out[e * fold : (e + 1) * fold, :] = fin[e]
+    combine()
     for copy in far:
         copy.wait_recv()
     for d in range(S - 1):
@@ -501,6 +499,10 @@
         copy.start()
         small.append(copy)
     square = ss[...]
+    for copy in ff:
+        copy.wait_recv()
+    for e in range(D):
+        a_out[e * fold : (e + 1) * fold, :] = fin[e]
     for i, copy in enumerate(small):
         copy.wait_recv()
         square = square + ssin[i]

time: 129 us -> 130 us (level)
  no operation moved by 1% of the time
where the time goes in v4:
time: 130 us; the launch traced here: 129 us
  Pallas kernels  116 us (89%)
  local copies, waits for them, and re-layouts  9.56 us (7%)
  other arithmetic  3.19 us (2%)
    pallas_call x1, Pallas kernels, fused(): pl.pallas_call(functools.partial(fused_kernel, (D, G, S, T, K)), out_shap...  116 us
    unnamed x4, local copies, waits for them, and re-layouts  3.28 us
    reshape x1, local copies, waits for them, and re-layouts, fused(): weight = jnp.transpose(proj_weight.reshape(G, fg, C), (0, 2, 1))  2.95 us

profile of v4, /device:TPU:0, one launch (start us, length us, event | category | flops | bytes accessed | tf_op | source)
XLA Modules:
  0.0 129.3 jit_solution(17035658983046684068)
XLA Ops:
  0.7 0.8 reshape.74.bt_ref
  1.4 0.0 copy-start
  1.4 0.8 add_bitcast_fusion
  2.2 0.2 convert_reduce_fusion
  2.4 0.7 multiply_add_fusion
  3.1 0.6 select_reduce_fusion.src_ref
  3.7 0.6 pad.4.plan_ref
  4.3 1.3 %broadcast_in_dim.16.qg_ref = f32[1,1536]{1,0:T(1,128)} reshape(f32[1536]{0:T(1024)} %param.12) | data formatting | bytes 12288 | tf_op jit(solution)/shard_map/broadcast_in_dim | solution.py:573
  5.6 0.7 broadcast_in_dim.19.want_ref
  6.3 0.9 multiply_sine_fusion
  7.2 3.0 %copy.16 = bf16[66,2,8,896]{3,2,0,1:T(8,128)(2,1)} copy(bf16[66,2,8,896]{3,2,1,0:T(8,128)(2,1)} %bitcast.18) | data formatting | bytes 3784704 | tf_op jit(solution)/shard_map/reshape | solution.py:572
  10.1 0.0 copy-done
  10.1 115.9 %shard_map.113 = (bf16[384,384]{1,0:T(8,128)(2,1)}, bf16[128,512]{1,0:T(8,128)(2,1)}) custom-call(bf16[2,528,896]{2,1,0:T(8,128)(2,1)} %bitcast.17, bf16[384,1792]{1,0:T(8,128)(2,1)} %x_ref.1, f32[1,1536]{1,0:T(1,128)} %broadcast_in_dim.16.qg_ref, f32[1,512]{1,0:T(1,128)} %bitcast.20, f32[96,64]{1,0:T(8,128)} %get-tuple-element.9.cos_ref, ...), custom_call_target="tpu_custom_call" | custom-call | tf_op jit(solution)/shard_map/pallas_call | solution.py:603
  126.0 1.7 %copy.19 = bf16[384,384]{1,0:T(8,128)(2,1)} copy(bf16[384,384]{1,0:T(8,128)(2,1)} %get-tuple-element.12) | data formatting | bytes 589824
  127.7 1.6 %copy.20 = bf16[4,32,512]{2,1,0:T(8,128)(2,1)} copy(bf16[4,32,512]{2,1,0:T(8,128)(2,1)} %bitcast.19) | data formatting | bytes 262144
  (4 shorter events, 0.0 us)
Async XLA Ops:
  1.4 8.7 %copy-start = (s32[32]{0:T(128)}, s32[32]{0:T(128)S(1)}, u32[]{:S(2)}) copy-start(s32[32]{0:T(128)S(1)} %reshape.74.bt_ref) | copy-start | bytes 388
